TPU v7x, 256 devices: a whole 4x4x8 slice. The times are simulated.
256 devices in a mesh: dom: 32 (over x, z), grp: 8 (over y, core).
Axes of the slice: x: 4, y: 4, z: 8, core: 2. Of those that a mesh axis runs over, the one named last changes fastest.
Arguments:
- node_feats: bfloat16 [65536, 1024], P(('dom', 'grp')), may hold values from -6 to 6
- weight: bfloat16 [1024, 512], replicated, may hold values from -0.1875 to 0.1875
- bias: float32 [512], replicated, may hold values from -4 to 4
- cotangent: bfloat16 [65536, 512], P(('dom', 'grp')), may hold values from -6 to 6
- tile_bank: bfloat16 [16, 128, 128], replicated, may hold values from -0.125 to 0.125
- local_cols: int32 [32, 16, 16], P('dom'), may hold values from 0 to 15
- local_banks: int32 [32, 16, 16], P('dom'), may hold values from 0 to 15
- published: int32 [32, 4], P('dom'), may hold values from 0 to 15, as said below
- send_table: int32 [32, 32, 2], replicated, may hold values from -1 to 3, as said below
- halo_rows: int32 [32, 32, 2], P('dom'), may hold values from 0 to 15
- halo_banks: int32 [32, 32, 2], P('dom'), may hold values from 0 to 15
Outputs:
- activations: bfloat16 [65536, 512], P(('dom', 'grp'))
- grad_nodes: bfloat16 [65536, 1024], P(('dom', 'grp'))
- grad_weight: float32 [1024, 512], replicated
- grad_bias: float32 [512], replicated
Inputs may be any that keep to these rules, and one draw needn't show every extreme that they name: `published`: the 4 entries of a partition are distinct block numbers of that partition; 0 and 15 each appear in some partition's list. `send_table`: entry s of the pair (src, p) is -1 or an index into the offered list of src; the live entries of a pair come first and are distinct; a pair (p, p) has none; some pair has all 2 entries live.
All inputs are finite; a program needn't handle non-finite values.
Results may differ from a plain program's by a relative error of at most 0.019.
The roundings to bfloat16 on the way count: a program that leaves them out, or rounds other values in their place, can miss the bound.
Values may be sent and summed in bfloat16 or wider, within the bound.
A program may use at most 64 MiB of HBM per device.

v0:
```python
import jax
import jax.numpy as jnp
from jax import lax
from jax.sharding import PartitionSpec as P


def per_device(
    node_feats,
    weight,
    bias,
    cotangent,
    tile_bank,
    local_cols,
    local_banks,
    published,
    send_table,
    halo_rows,
    halo_banks,
):
    domains = lax.axis_size("dom")
    groups = lax.axis_size("grp")
    domain_index = lax.axis_index("dom")
    rows_here = node_feats.shape[0]
    tile_size = tile_bank.shape[1]
    slot_count = send_table.shape[2]
    pub_count = published.shape[1]
    tiles_row = local_cols.shape[2]
    features = lax.all_to_all(node_feats, "grp", split_axis=1, concat_axis=0, tiled=True)
    part_rows, narrow = features.shape
    blocks = part_rows // tile_size
    feat_blocks = features.reshape(blocks, tile_size, narrow)
    cols_here = local_cols[0]
    banks_here = local_banks[0]
    own_pub = published[0]
    incoming = lax.dynamic_index_in_dim(send_table, domain_index, 1, keepdims=False)
    live_in = (incoming >= 0).astype(jnp.float32)[:, :, None, None]
    rows_in = halo_rows[0]
    halo_tiles = tile_bank[halo_banks[0]]
    source_ids = lax.broadcasted_iota(jnp.int32, (domains, slot_count), 0)
    gathered_ids = source_ids * pub_count + jnp.maximum(incoming, 0)

    def forward_tiles(position, running):
        column = lax.dynamic_index_in_dim(cols_here, position, 1, keepdims=False)
        bank_ids = lax.dynamic_index_in_dim(banks_here, position, 1, keepdims=False)
        return running + jnp.einsum(
            "rij,rjf->rif",
            tile_bank[bank_ids],
            feat_blocks[column],
            preferred_element_type=jnp.float32,
        )

    running = lax.fori_loop(
        0, tiles_row, forward_tiles, jnp.zeros((blocks, tile_size, narrow), jnp.float32)
    )
    shared = feat_blocks[own_pub]
    everyone = lax.all_gather(shared, "dom", axis=0, tiled=True)
    remote = everyone[gathered_ids]
    halo_terms = (
        jnp.einsum("dsij,dsjf->dsif", halo_tiles, remote, preferred_element_type=jnp.float32)
        * live_in
    )
    running = running + jax.ops.segment_sum(
        halo_terms.reshape(domains * slot_count, tile_size, narrow),
        rows_in.reshape(-1),
        num_segments=blocks,
    )
    agg_narrow = running.astype(jnp.bfloat16).reshape(part_rows, narrow)
    aggregated = lax.all_to_all(agg_narrow, "grp", split_axis=0, concat_axis=1, tiled=True)
    pre_act = jnp.dot(aggregated, weight, preferred_element_type=jnp.float32) + bias
    activations = jnp.maximum(pre_act, 0.0).astype(jnp.bfloat16)
    grad_pre = jnp.where(pre_act > 0, cotangent.astype(jnp.float32), 0.0).astype(jnp.bfloat16)
    weight_part = lax.dot_general(
        aggregated, grad_pre, (((0,), (0,)), ((), ())), preferred_element_type=jnp.float32
    )
    bias_part = jnp.sum(grad_pre.astype(jnp.float32), axis=0)
    grad_agg = lax.dot_general(
        grad_pre, weight, (((1,), (1,)), ((), ())), preferred_element_type=jnp.float32
    ).astype(jnp.bfloat16)
    grad_narrow = lax.all_to_all(grad_agg, "grp", split_axis=1, concat_axis=0, tiled=True)
    grad_blocks = grad_narrow.reshape(blocks, tile_size, narrow)

    def backward_tiles(position, running):
        column = lax.dynamic_index_in_dim(cols_here, position, 1, keepdims=False)
        bank_ids = lax.dynamic_index_in_dim(banks_here, position, 1, keepdims=False)
        contrib = jnp.einsum(
            "rji,rjf->rif", tile_bank[bank_ids], grad_blocks, preferred_element_type=jnp.float32
        )
        return running + jax.ops.segment_sum(contrib, column, num_segments=blocks)

    grad_total = lax.fori_loop(
        0, tiles_row, backward_tiles, jnp.zeros((blocks, tile_size, narrow), jnp.float32)
    )
    back_terms = (
        jnp.einsum(
            "dsji,dsjf->dsif", halo_tiles, grad_blocks[rows_in], preferred_element_type=jnp.float32
        )
        * live_in
    )
    placed = jax.ops.segment_sum(
        back_terms.reshape(domains * slot_count, tile_size, narrow),
        gathered_ids.reshape(-1),
        num_segments=domains * pub_count,
    )
    mine_back = lax.psum_scatter(placed, "dom", scatter_dimension=0, tiled=True)
    back_total = jax.ops.segment_sum(mine_back, own_pub, num_segments=blocks)
    grad_total = grad_total + back_total
    grad_nodes = lax.all_to_all(
        grad_total.astype(jnp.bfloat16).reshape(part_rows, narrow),
        "grp",
        split_axis=0,
        concat_axis=1,
        tiled=True,
    )
    norm_scale = float(rows_here * groups * domains) ** (-0.5)
    weight_total, bias_total = lax.psum((weight_part, bias_part), ("dom", "grp"))
    return (activations, grad_nodes, weight_total * norm_scale, bias_total * norm_scale)


def solution(mesh):
    in_specs = (
        P(("dom", "grp"), None),
        P(),
        P(),
        P(("dom", "grp"), None),
        P(),
        P("dom", None, None),
        P("dom", None, None),
        P("dom", None),
        P(),
        P("dom", None, None),
        P("dom", None, None),
    )
    out_specs = (P(("dom", "grp"), None), P(("dom", "grp"), None), P(), P())
    return jax.shard_map(
        per_device, mesh=mesh, in_specs=in_specs, out_specs=out_specs, check_vma=False
    )
```

profile of v0, /device:TPU:2, one launch (start us, length us, event | category | flops | bytes accessed | tf_op | source)
XLA Modules:
  0.0 686.9 jit_solution(15913844381797116386)
XLA Ops:
  9.3 4.5 all-to-all-start
  17.1 7.1 %all-to-all-done = bf16[256,8,128]{2,0,1:T(8,128)(2,1)} async-done(((bf16[256,8,128]{2,0,1:T(8,128)(2,1)}), bf16[256,8,128]{2,0,1:T(8,128)(2,1)}, u32[]{:S(2)}, u32[]{:S(2)}) %all-to-all-start) | async-done | bytes 524320 | tf_op jit(solution)/shard_map/all_to_all | solution.py:28
  26.5 74.0 %while.28 = (s32[]{:T(128)}, f32[16,128,128]{2,1,0:T(8,128)S(1)}, s32[16,16]{0,1:T(8,128)S(1)}, bf16[16,128,128]{2,1,0:T(8,128)(2,1)S(1)}, s32[16,16]{0,1:T(8,12...) while((s32[]{:T(128)}, f32[16,128,128]{2,1,0:T(8,128)S(1)}, ...), condition=%wide.region_1.2_spmd.clone, body=%wide.region_0.1_spmd.clone.sunk | while | flops 67635296 | bytes 5251683 | solution.py:52
  100.5 7.6 %all-gather.3.cloned.1.call-done = bf16[128,128,128]{2,1,0:T(8,128)(2,1)} async-done(((bf16[4,128,128]{2,1,0:T(8,128)(2,1)}), bf16[128,128,128]{2,1,0:T(8,128)(2,1)}) %all-gather.3.cloned.1.call-update) | async-done | bytes 4194320 | tf_op jit(solution)/shard_map/all_gather | solution.py:56
  108.1 4.3 gather_fusion.5
  112.4 4.9 convolution_multiply_fusion.1
  117.2 8.8 %scatter_fusion.1 = f32[16,128,128]{2,1,0:T(8,128)S(1)} fusion(f32[16,128,128]{2,1,0:T(8,128)S(1)} %get-tuple-element.222, s32[64]{0:T(128)S(1)} %reshape.272, f32[64,128,128]{2,1,0:T(8,128)} %bitcast.94), kind=kCustom, calls=%fused_computation.8 | custom fusion | flops 1048576 | bytes 12583168 | tf_op jit(solution)/shard_map/scatter-add | solution.py:62
  126.9 4.4 all-to-all-start.1
  131.6 10.1 %all-to-all-done.1 = bf16[8,256,128]{2,1,0:T(8,128)(2,1)S(1)} async-done(((bf16[8,256,128]{2,1,0:T(8,128)(2,1)}), bf16[8,256,128]{2,1,0:T(8,128)(2,1)S(1)}, u32[]{:S(2)}, u32[]{:S(2)}) %all-to-all-start.1) | async-done | bytes 524320 | tf_op jit(solution)/shard_map/all_to_all | solution.py:68
  144.6 3.5 all-to-all-start.2
  148.6 9.8 %all-to-all-done.2 = bf16[256,8,128]{2,0,1:T(8,128)(2,1)S(1)} async-done(((bf16[256,8,128]{2,0,1:T(8,128)(2,1)}), bf16[256,8,128]{2,0,1:T(8,128)(2,1)S(1)}, u32[]{:S(2)}, u32[]{:S(2)}) %all-to-all-start.2) | async-done | bytes 524320 | tf_op jit(solution)/shard_map/all_to_all | solution.py:79
  160.5 5.2 convolution_multiply_fusion
  165.8 4.3 broadcast_in_dim.12
  170.0 13.4 %scatter_fusion.2 = f32[128,128,128]{2,1,0:T(8,128)} fusion(f32[128,128,128]{2,1,0:T(8,128)} %broadcast_in_dim.12, s32[64]{0:T(128)S(1)} %add_bitcast_fusion, f32[64,128,128]{2,1,0:T(8,128)} %bitcast.93), kind=kCustom, calls=%fused_computation.9 | custom fusion | flops 1048576 | bytes 12583168 | tf_op jit(solution)/shard_map/scatter-add | solution.py:99
  183.5 75.8 %psum.15 = f32[512]{0:T(512)S(1)} all-reduce(f32[512]{0:T(512)S(1)} %get-tuple-element.277), channel_id=1, replica_groups=mesh['dom'=32,'grp'=8] {'dom','grp'}, use_global_device_ids=true, to_apply=%region_11.12 | all-reduce | flops 512 | bytes 4096 | tf_op jit(solution)/shard_map/psum | solution.py:115
  262.2 98.2 %while.27 = (s32[]{:T(128)}, f32[16,128,128]{2,1,0:T(8,128)}, s32[16,16]{0,1:T(8,128)S(1)}, s32[16,16]{0,1:T(8,128)S(1)}, bf16[16,128,128]{2,1,0:T(8,128)(2,1)S(...) while((s32[]{:T(128)}, f32[16,128,128]{2,1,0:T(8,128)}, s32[16,16]{0,1:T(8,128)S(1)}, ...), condition=%wide.region_5.6_spmd, body=%wide.region_3.5_spmd.sunk | while | flops 67372080 | bytes 6296081 | solution.py:90
  265.0 3.3 scatter_fusion
  283.4 3.3 scatter_fusion
  289.6 3.3 scatter_fusion
  301.9 3.3 scatter_fusion
  320.3 3.4 scatter_fusion
  360.4 48.2 %reduce-scatter.2.cloned.1.call-done = f32[4,128,128]{2,1,0:T(8,128)} async-done(((f32[128,128,128]{2,1,0:T(8,128)}), f32[4,128,128]{2,1,0:T(8,128)}) %reduce-scatter.2.cloned.1.call-update) | async-done | bytes 262160 | tf_op jit(solution)/shard_map/reduce_scatter | solution.py:104
  413.3 4.3 all-to-all-start.3
  418.1 257.9 %all-reduce.2.cloned.1.call-done = f32[1024,512]{1,0:T(8,128)} async-done(((f32[1024,512]{1,0:T(8,128)}), f32[1024,512]{1,0:T(8,128)}) %all-reduce.2.cloned.1.call-update) | async-done | bytes 2097168 | tf_op jit(solution)/shard_map/psum | solution.py:115
  (246 shorter events, 181.0 us)
Async XLA Ops:
  7.2 134.8 %copy-start = (bf16[1024,512]{1,0:T(8,128)(2,1)S(1)}, bf16[1024,512]{1,0:T(8,128)(2,1)}, u32[]{:S(2)}) copy-start(bf16[1024,512]{1,0:T(8,128)(2,1)} %param.16) | copy-start | bytes 3145732
  7.2 6.6 copy-start.3
  7.2 6.8 copy-start.8
  7.2 7.4 %copy-start.4 = (s32[1,16,16]{2,1,0:T(8,128)S(1)}, s32[1,16,16]{2,1,0:T(8,128)}, u32[]{:S(2)}) copy-start(s32[1,16,16]{2,1,0:T(8,128)} %param.21) | copy-start | bytes 3076
  7.2 7.4 %copy-start.5 = (s32[1,16,16]{2,1,0:T(8,128)S(1)}, s32[1,16,16]{2,1,0:T(8,128)}, u32[]{:S(2)}) copy-start(s32[1,16,16]{2,1,0:T(8,128)} %param.20) | copy-start | bytes 3076
  7.2 7.5 %copy-start.6 = (s32[1,32,2]{1,2,0:T(2,128)S(1)}, s32[1,32,2]{1,2,0:T(2,128)}, u32[]{:S(2)}) copy-start(s32[1,32,2]{1,2,0:T(2,128)} %param.24) | copy-start | bytes 772
  7.2 7.7 %copy-start.1 = (bf16[16,128,128]{2,1,0:T(8,128)(2,1)S(1)}, bf16[16,128,128]{2,1,0:T(8,128)(2,1)}, u32[]{:S(2)}) copy-start(bf16[16,128,128]{2,1,0:T(8,128)(2,1)} %param.19) | copy-start | bytes 1572868
  9.3 14.9 %all-to-all-start = ((bf16[256,8,128]{2,0,1:T(8,128)(2,1)}), bf16[256,8,128]{2,0,1:T(8,128)(2,1)}, u32[]{:S(2)}, u32[]{:S(2)}) async-start(bf16[256,8,128]{2,0,1:T(8,128)(2,1)} %copy_bitcast_fusion.1), calls=%async_computation | async-start | bytes 1048576 | tf_op jit(solution)/shard_map/all_to_all | solution.py:28
  13.8 94.3 %all-gather.3.cloned.1.call-start = ((), (), s32[]{:S(2)}) async-start(), calls=%async_computation.7 | async-start | bytes 4325376 | tf_op jit(solution)/shard_map/all_gather | solution.py:56
  14.9 2.2 copy-start.9
  126.0 15.9 %copy-start.7 = (f32[512]{0:T(512)S(1)}, f32[512]{0:T(512)}, u32[]{:S(2)}) copy-start(f32[512]{0:T(512)} %param.17) | copy-start | bytes 6148
  126.9 16.2 %copy-start.2 = (bf16[256,512]{1,0:T(8,128)(2,1)S(1)}, bf16[256,512]{1,0:T(8,128)(2,1)}, u32[]{:S(2)}) copy-start(bf16[256,512]{1,0:T(8,128)(2,1)} %param.18) | copy-start | bytes 786436
  126.9 14.8 %all-to-all-start.1 = ((bf16[8,256,128]{2,1,0:T(8,128)(2,1)}), bf16[8,256,128]{2,1,0:T(8,128)(2,1)S(1)}, u32[]{:S(2)}, u32[]{:S(2)}) async-start(bf16[8,256,128]{2,1,0:T(8,128)(2,1)} %bitcast.15), calls=%async_computation.1 | async-start | bytes 1048576 | tf_op jit(solution)/shard_map/all_to_all | solution.py:68
  144.6 13.8 %all-to-all-start.2 = ((bf16[256,8,128]{2,0,1:T(8,128)(2,1)}), bf16[256,8,128]{2,0,1:T(8,128)(2,1)S(1)}, u32[]{:S(2)}, u32[]{:S(2)}) async-start(bf16[256,8,128]{2,0,1:T(8,128)(2,1)} %bitcast.76), calls=%async_computation.2 | async-start | bytes 1048576 | tf_op jit(solution)/shard_map/all_to_all | solution.py:79
  148.1 260.6 %reduce-scatter.2.cloned.1.call-start = ((), (), s32[]{:S(2)}) async-start(), calls=%async_computation.5 | async-start | bytes 8650752 | tf_op jit(solution)/shard_map/reduce_scatter | solution.py:104
  183.5 492.5 %all-reduce.2.cloned.1.call-start = ((), (), s32[]{:S(2)}) async-start(), calls=%async_computation.6 | async-start | bytes 4194304 | tf_op jit(solution)/shard_map/psum | solution.py:115
  413.3 265.9 %all-to-all-start.3 = ((bf16[8,256,128]{2,1,0:T(8,128)(2,1)}), bf16[8,256,128]{2,1,0:T(8,128)(2,1)S(1)}, u32[]{:S(2)}, u32[]{:S(2)}) async-start(bf16[8,256,128]{2,1,0:T(8,128)(2,1)} %bitcast.26), calls=%async_computation.4 | async-start | bytes 1048576 | tf_op jit(solution)/shard_map/all_to_all | solution.py:107
Sparse Core Ops, SparseCore 0:
  26.6 81.3 all-gather.2
  183.6 225.0 reduce-scatter.1
  415.5 260.4 all-reduce.1
where the time goes:
time: 691 us; the launch traced here: 687 us
  waiting for transfers between devices  341 us (49%)
  local copies, waits for them, and re-layouts  94.3 us (14%)
  other arithmetic  85.3 us (12%)
  blocking collectives  75.8 us (11%)
  matrix products  58.9 us (9%)
  starting transfers between devices  16.8 us (2%)
  between operations  14 us (2%)
    psum x1, waiting for transfers between devices, per_device(): lax.psum((weight_part, bias_part), ('dom', 'grp'))  258 us
    psum x1, blocking collectives, per_device(): lax.psum((weight_part, bias_part), ('dom', 'grp'))  75.8 us
    scatter-add x16, other arithmetic, backward_tiles(): return running + jax.ops.segment_sum(contrib, column, num_segments=blocks)  53.1 us
    reduce_scatter x1, waiting for transfers between devices, per_device(): mine_back = lax.psum_scatter(placed, 'dom', scatter_dimension=0, tiled=True)  48.2 us
    gather x16, local copies, waits for them, and re-layouts, forward_tiles(): feat_blocks[column]  39.2 us
    dot_general x16, matrix products, forward_tiles(): jnp.einsum('rij,rjf->rif', tile_bank[bank_ids], feat_blocks[column], pref...  23.2 us
    gather x16, local copies, waits for them, and re-layouts, backward_tiles(): tile_bank[bank_ids]  22.5 us
    dot_general x16, matrix products, backward_tiles(): jnp.einsum('rji,rjf->rif', tile_bank[bank_ids], grad_blocks, preferred_el...  22.3 us
  transfers between devices with their start and end apart: 7, of which 6 were waited for; matrix products, arithmetic and copies ran while one was open for 27% of the time, Pallas kernels for 0%

commit v1 on v0

--- a/solution.py
+++ b/solution.py
@@ -2,6 +2,7 @@
 import jax.numpy as jnp
 from jax import lax
 from jax.sharding import PartitionSpec as P
+from jax.lax import all_to_all, axis_size
 
 
 def per_device(
@@ -65,7 +66,10 @@
         num_segments=blocks,
     )
     agg_narrow = running.astype(jnp.bfloat16).reshape(part_rows, narrow)
-    aggregated = lax.all_to_all(agg_narrow, "grp", split_axis=0, concat_axis=1, tiled=True)
+    update_waves = lambda load: jnp.concatenate(
+        all_to_all(jnp.stack(jnp.split(load, axis_size("grp"), axis=0)), "grp", 0, 0), axis=1
+    )
+    aggregated = update_waves(agg_narrow)
     pre_act = jnp.dot(aggregated, weight, preferred_element_type=jnp.float32) + bias
     activations = jnp.maximum(pre_act, 0.0).astype(jnp.bfloat16)
     grad_pre = jnp.where(pre_act > 0, cotangent.astype(jnp.float32), 0.0).astype(jnp.bfloat16)

time: 691 us -> 696 us (level)
  no operation moved by 1% of the time
where the time goes in v1:
time: 696 us; the launch traced here: 692 us
  waiting for transfers between devices  341 us (49%)
  local copies, waits for them, and re-layouts  100 us (14%)
  other arithmetic  84.9 us (12%)
  blocking collectives  75.7 us (11%)
  matrix products  58.9 us (8%)
  starting transfers between devices  16.7 us (2%)
  between operations  14.1 us (2%)
    psum x1, waiting for transfers between devices, per_device(): lax.psum((weight_part, bias_part), ('dom', 'grp'))  258 us
    psum x1, blocking collectives, per_device(): lax.psum((weight_part, bias_part), ('dom', 'grp'))  75.7 us
    scatter-add x16, other arithmetic, backward_tiles(): return running + jax.ops.segment_sum(contrib, column, num_segments=blocks)  53.5 us
    reduce_scatter x1, waiting for transfers between devices, per_device(): mine_back = lax.psum_scatter(placed, 'dom', scatter_dimension=0, tiled=True)  47.9 us
    gather x16, local copies, waits for them, and re-layouts, forward_tiles(): feat_blocks[column]  39.2 us
    dot_general x16, matrix products, forward_tiles(): jnp.einsum('rij,rjf->rif', tile_bank[bank_ids], feat_blocks[column], pref...  23.2 us
    gather x16, local copies, waits for them, and re-layouts, backward_tiles(): tile_bank[bank_ids]  22.5 us
    dot_general x16, matrix products, backward_tiles(): jnp.einsum('rji,rjf->rif', tile_bank[bank_ids], grad_blocks, preferred_el...  22.3 us
  transfers between devices with their start and end apart: 7, of which 6 were waited for; matrix products, arithmetic and copies ran while one was open for 27% of the time, Pallas kernels for 0%

profile of v1, /device:TPU:2, one launch (start us, length us, event | category | flops | bytes accessed | tf_op | source)
XLA Modules:
  0.0 692.0 jit_solution(1476065796759474951)
XLA Ops:
  9.3 4.5 all-to-all-start
  17.1 7.1 %all-to-all-done = bf16[256,8,128]{2,0,1:T(8,128)(2,1)} async-done(((bf16[256,8,128]{2,0,1:T(8,128)(2,1)}), bf16[256,8,128]{2,0,1:T(8,128)(2,1)}, u32[]{:S(2)}, u32[]{:S(2)}) %all-to-all-start) | async-done | bytes 524320 | tf_op jit(solution)/shard_map/all_to_all | solution.py:29
  26.5 74.0 %while.28 = (s32[]{:T(128)}, f32[16,128,128]{2,1,0:T(8,128)S(1)}, s32[16,16]{0,1:T(8,128)S(1)}, bf16[16,128,128]{2,1,0:T(8,128)(2,1)S(1)}, s32[16,16]{0,1:T(8,12...) while((s32[]{:T(128)}, f32[16,128,128]{2,1,0:T(8,128)S(1)}, ...), condition=%wide.region_1.2_spmd.clone, body=%wide.region_0.1_spmd.clone.sunk | while | flops 67635296 | bytes 5251683 | solution.py:53
  100.5 7.6 %all-gather.3.cloned.1.call-done = bf16[128,128,128]{2,1,0:T(8,128)(2,1)} async-done(((bf16[4,128,128]{2,1,0:T(8,128)(2,1)}), bf16[128,128,128]{2,1,0:T(8,128)(2,1)}) %all-gather.3.cloned.1.call-update) | async-done | bytes 4194320 | tf_op jit(solution)/shard_map/all_gather | solution.py:57
  108.1 4.3 gather_fusion.5
  112.4 4.9 convolution_multiply_fusion.1
  117.3 8.8 %scatter_fusion.1 = f32[16,128,128]{2,1,0:T(8,128)S(1)} fusion(f32[16,128,128]{2,1,0:T(8,128)S(1)} %get-tuple-element.222, s32[64]{0:T(128)S(1)} %reshape.292, f32[64,128,128]{2,1,0:T(8,128)} %bitcast.102), kind=kCustom, calls=%fused_computation.8 | custom fusion | flops 1048576 | bytes 12583168 | tf_op jit(solution)/shard_map/scatter-add | solution.py:63
  132.2 4.3 all-to-all-start.1
  136.7 10.1 %all-to-all-done.1 = bf16[8,256,128]{1,2,0:T(8,128)(2,1)S(1)} async-done(((bf16[8,256,128]{1,2,0:T(8,128)(2,1)}), bf16[8,256,128]{1,2,0:T(8,128)(2,1)S(1)}, u32[]{:S(2)}, u32[]{:S(2)}) %all-to-all-start.1) | async-done | bytes 524320 | tf_op jit(solution)/shard_map/all_to_all | solution.py:70
  149.5 3.5 all-to-all-start.2
  153.5 9.8 %all-to-all-done.2 = bf16[256,8,128]{2,0,1:T(8,128)(2,1)S(1)} async-done(((bf16[256,8,128]{2,0,1:T(8,128)(2,1)}), bf16[256,8,128]{2,0,1:T(8,128)(2,1)S(1)}, u32[]{:S(2)}, u32[]{:S(2)}) %all-to-all-start.2) | async-done | bytes 524320 | tf_op jit(solution)/shard_map/all_to_all | solution.py:83
  165.4 5.2 convolution_multiply_fusion
  170.6 4.3 broadcast_in_dim.12
  174.9 13.4 %scatter_fusion.2 = f32[128,128,128]{2,1,0:T(8,128)} fusion(f32[128,128,128]{2,1,0:T(8,128)} %broadcast_in_dim.12, s32[64]{0:T(128)S(1)} %add_bitcast_fusion, f32[64,128,128]{2,1,0:T(8,128)} %bitcast.101), kind=kCustom, calls=%fused_computation.9 | custom fusion | flops 1048576 | bytes 12583168 | tf_op jit(solution)/shard_map/scatter-add | solution.py:103
  188.4 75.7 %psum.15 = f32[512]{0:T(512)S(1)} all-reduce(f32[512]{0:T(512)S(1)} %get-tuple-element.277), channel_id=1, replica_groups=mesh['dom'=32,'grp'=8] {'dom','grp'}, use_global_device_ids=true, to_apply=%region_11.12 | all-reduce | flops 512 | bytes 4096 | tf_op jit(solution)/shard_map/psum | solution.py:119
  267.0 98.7 %while.27 = (s32[]{:T(128)}, f32[16,128,128]{2,1,0:T(8,128)}, s32[16,16]{0,1:T(8,128)S(1)}, s32[16,16]{0,1:T(8,128)S(1)}, bf16[16,128,128]{2,1,0:T(8,128)(2,1)S(...) while((s32[]{:T(128)}, f32[16,128,128]{2,1,0:T(8,128)}, s32[16,16]{0,1:T(8,128)S(1)}, ...), condition=%wide.region_5.6_spmd, body=%wide.region_3.5_spmd.sunk | while | flops 67372080 | bytes 6296081 | solution.py:94
  269.9 3.4 scatter_fusion
  288.4 3.4 scatter_fusion
  294.6 3.4 scatter_fusion
  313.2 3.4 scatter_fusion
  325.5 3.4 scatter_fusion
  365.7 47.9 %reduce-scatter.2.cloned.1.call-done = f32[4,128,128]{2,1,0:T(8,128)} async-done(((f32[128,128,128]{2,1,0:T(8,128)}), f32[4,128,128]{2,1,0:T(8,128)}) %reduce-scatter.2.cloned.1.call-update) | async-done | bytes 262160 | tf_op jit(solution)/shard_map/reduce_scatter | solution.py:108
  418.2 4.3 all-to-all-start.3
  423.1 258.0 %all-reduce.2.cloned.1.call-done = f32[1024,512]{1,0:T(8,128)} async-done(((f32[1024,512]{1,0:T(8,128)}), f32[1024,512]{1,0:T(8,128)}) %all-reduce.2.cloned.1.call-update) | async-done | bytes 2097168 | tf_op jit(solution)/shard_map/psum | solution.py:119
  (262 shorter events, 186.2 us)
Async XLA Ops:
  7.2 139.7 %copy-start = (bf16[1024,512]{1,0:T(8,128)(2,1)S(1)}, bf16[1024,512]{1,0:T(8,128)(2,1)}, u32[]{:S(2)}) copy-start(bf16[1024,512]{1,0:T(8,128)(2,1)} %param.16) | copy-start | bytes 3145732
  7.2 6.6 copy-start.3
  7.2 6.8 copy-start.8
  7.2 7.4 %copy-start.4 = (s32[1,16,16]{2,1,0:T(8,128)S(1)}, s32[1,16,16]{2,1,0:T(8,128)}, u32[]{:S(2)}) copy-start(s32[1,16,16]{2,1,0:T(8,128)} %param.21) | copy-start | bytes 3076
  7.2 7.4 %copy-start.5 = (s32[1,16,16]{2,1,0:T(8,128)S(1)}, s32[1,16,16]{2,1,0:T(8,128)}, u32[]{:S(2)}) copy-start(s32[1,16,16]{2,1,0:T(8,128)} %param.20) | copy-start | bytes 3076
  7.2 7.5 %copy-start.6 = (s32[1,32,2]{1,2,0:T(2,128)S(1)}, s32[1,32,2]{1,2,0:T(2,128)}, u32[]{:S(2)}) copy-start(s32[1,32,2]{1,2,0:T(2,128)} %param.24) | copy-start | bytes 772
  7.2 7.7 %copy-start.1 = (bf16[16,128,128]{2,1,0:T(8,128)(2,1)S(1)}, bf16[16,128,128]{2,1,0:T(8,128)(2,1)}, u32[]{:S(2)}) copy-start(bf16[16,128,128]{2,1,0:T(8,128)(2,1)} %param.19) | copy-start | bytes 1572868
  9.3 14.9 %all-to-all-start = ((bf16[256,8,128]{2,0,1:T(8,128)(2,1)}), bf16[256,8,128]{2,0,1:T(8,128)(2,1)}, u32[]{:S(2)}, u32[]{:S(2)}) async-start(bf16[256,8,128]{2,0,1:T(8,128)(2,1)} %copy_bitcast_fusion.1), calls=%async_computation | async-start | bytes 1048576 | tf_op jit(solution)/shard_map/all_to_all | solution.py:29
  13.8 94.3 %all-gather.3.cloned.1.call-start = ((), (), s32[]{:S(2)}) async-start(), calls=%async_computation.7 | async-start | bytes 4325376 | tf_op jit(solution)/shard_map/all_gather | solution.py:57
  14.9 2.2 copy-start.9
  126.1 20.7 %copy-start.7 = (f32[512]{0:T(512)S(1)}, f32[512]{0:T(512)}, u32[]{:S(2)}) copy-start(f32[512]{0:T(512)} %param.17) | copy-start | bytes 6148
  128.4 19.6 %copy-start.2 = (bf16[256,512]{1,0:T(8,128)(2,1)S(1)}, bf16[256,512]{1,0:T(8,128)(2,1)}, u32[]{:S(2)}) copy-start(bf16[256,512]{1,0:T(8,128)(2,1)} %param.18) | copy-start | bytes 786436
  132.2 14.6 %all-to-all-start.1 = ((bf16[8,256,128]{1,2,0:T(8,128)(2,1)}), bf16[8,256,128]{1,2,0:T(8,128)(2,1)S(1)}, u32[]{:S(2)}, u32[]{:S(2)}) async-start(bf16[8,256,128]{1,2,0:T(8,128)(2,1)} %constant_dynamic-update-slice_fusion), calls=%async_computation.1 | async-start | bytes 1048576 | tf_op jit(solution)/shard_map/all_to_all | solution.py:70
  149.5 13.8 %all-to-all-start.2 = ((bf16[256,8,128]{2,0,1:T(8,128)(2,1)}), bf16[256,8,128]{2,0,1:T(8,128)(2,1)S(1)}, u32[]{:S(2)}, u32[]{:S(2)}) async-start(bf16[256,8,128]{2,0,1:T(8,128)(2,1)} %bitcast.84), calls=%async_computation.2 | async-start | bytes 1048576 | tf_op jit(solution)/shard_map/all_to_all | solution.py:83
  153.0 260.6 %reduce-scatter.2.cloned.1.call-start = ((), (), s32[]{:S(2)}) async-start(), calls=%async_computation.5 | async-start | bytes 8650752 | tf_op jit(solution)/shard_map/reduce_scatter | solution.py:108
  188.4 492.7 %all-reduce.2.cloned.1.call-start = ((), (), s32[]{:S(2)}) async-start(), calls=%async_computation.6 | async-start | bytes 4194304 | tf_op jit(solution)/shard_map/psum | solution.py:119
  418.2 266.1 %all-to-all-start.3 = ((bf16[8,256,128]{2,1,0:T(8,128)(2,1)}), bf16[8,256,128]{2,1,0:T(8,128)(2,1)S(1)}, u32[]{:S(2)}, u32[]{:S(2)}) async-start(bf16[8,256,128]{2,1,0:T(8,128)(2,1)} %bitcast.33), calls=%async_computation.4 | async-start | bytes 1048576 | tf_op jit(solution)/shard_map/all_to_all | solution.py:111
Sparse Core Ops, SparseCore 0:
  26.6 81.3 all-gather.2
  188.5 225.0 reduce-scatter.1
  420.5 260.6 all-reduce.1
